TPU v7x, 768 devices: a whole 4x8x12 slice. The times are simulated.
768 devices in a mesh: seq: 64 (over y, x, core), head: 12 (over z).
Axes of the slice: x: 4, y: 8, z: 12, core: 2. Of those that a mesh axis runs over, the one named last changes fastest.
Arguments:
- query_act: bfloat16 [16384, 4608], P('seq', 'head'), may hold values from -0.59765625 to 0.59765625
- key_act: bfloat16 [16384, 4608], P('seq', 'head'), may hold values from -0.59765625 to 0.59765625
- value_act: bfloat16 [16384, 4608], P('seq', 'head'), may hold values from -0.59765625 to 0.59765625
- grad_output: bfloat16 [16384, 4608], P('seq', 'head'), may hold values from -0.375 to 0.375
- log_decay: float32 [16384, 36], P('seq', 'head'), may hold values from -1 to 0
- w_query: bfloat16 [6144, 4608], P(None, 'head'), may hold values from -0.0625 to 0.0625
- w_key: bfloat16 [6144, 4608], P(None, 'head'), may hold values from -0.0625 to 0.0625
Outputs:
- grad_input: bfloat16 [6144, 16384], P('head', 'seq')
All inputs are finite; a program needn't handle non-finite values.
Results may differ from a plain program's by a relative error of at most 0.015.
Values may be sent and summed in bfloat16 or wider, within the bound.
A program may use at most 128 MiB of HBM per device.

v0:
```python
import jax
import jax.numpy as jnp
from jax import lax
from jax.sharding import Mesh
from jax.sharding import PartitionSpec as P

SEQ = ("seq_0", "seq_1", "seq_2")


def nothing_yet(array, identity):
    return jax.tree.map(
        lambda a, e: jnp.broadcast_to(jnp.asarray(e, a.dtype), a.shape), array, identity
    )


def carried_in(array, axes, combine, identity, reverse):
    before = start = nothing_yet(array, identity)
    subtotal = array
    for axis in reversed(axes):
        size, place = (lax.axis_size(axis), lax.axis_index(axis))
        pieces = jax.tree.map(lambda part: lax.all_gather(part, axis), subtotal)
        inside, subtotal = (start, start)
        for k in reversed(range(size)) if reverse else range(size):
            passed = k > place if reverse else k < place
            subtotal = combine(subtotal, jax.tree.map(lambda part: part[k], pieces))
            inside = jax.tree.map(lambda new, old: jnp.where(passed, new, old), subtotal, inside)
        before = combine(inside, before)
    return before


def chain_combine(earlier, later):
    return (earlier[0] * later[0], later[0][:, None, None] * earlier[1] + later[1])


def shards(query_act, key_act, value_act, grad_output, log_decay, w_query, w_key):
    f32 = jnp.float32
    bf16 = jnp.bfloat16
    span = query_act.shape[0]
    nheads = log_decay.shape[1]
    width = query_act.shape[1] // nheads
    queries = query_act.reshape(span, nheads, width)
    keys_blk = key_act.reshape(span, nheads, width)
    values_blk = value_act.reshape(span, nheads, width)
    grads_blk = grad_output.reshape(span, nheads, width)
    cumlog = jnp.cumsum(log_decay, axis=0)
    last_log = cumlog[-1]
    decay_total = jnp.exp(last_log)
    key_weighted = (keys_blk * jnp.exp(last_log[None, :] - cumlog)[:, :, None]).astype(bf16)
    query_weighted = (queries * jnp.exp(cumlog)[:, :, None]).astype(bf16)
    local_state = jnp.einsum("thd,the->hde", key_weighted, values_blk, preferred_element_type=f32)
    local_grad = jnp.einsum("thd,the->hde", query_weighted, grads_blk, preferred_element_type=f32)
    identity = (jnp.ones_like(decay_total), jnp.zeros_like(local_state))
    state_in = carried_in((decay_total, local_state), SEQ, chain_combine, identity, False)[1]
    grad_in = carried_in((decay_total, local_grad), SEQ, chain_combine, identity, True)[1]
    positions = jnp.arange(span)
    causal_mask = positions[:, None] >= positions[None, :]
    log_gap = cumlog[:, None, :] - cumlog[None, :, :]
    decay_mat = jnp.where(causal_mask[:, :, None], jnp.exp(jnp.minimum(log_gap, 0.0)), 0.0)
    dot_scores = jnp.einsum("the,she->tsh", grads_blk, values_blk, preferred_element_type=f32)
    weighted = (dot_scores * decay_mat).astype(bf16)
    dq_local = jnp.einsum("tsh,shd->thd", weighted, keys_blk, preferred_element_type=f32)
    dk_local = jnp.einsum("tsh,thd->shd", weighted, queries, preferred_element_type=f32)
    dq_carry = (
        jnp.einsum("the,hde->thd", grads_blk, state_in.astype(bf16), preferred_element_type=f32)
        * jnp.exp(cumlog)[:, :, None]
    )
    dk_carry = (
        jnp.einsum("the,hde->thd", values_blk, grad_in.astype(bf16), preferred_element_type=f32)
        * jnp.exp(last_log[None, :] - cumlog)[:, :, None]
    )
    dq_flat = (dq_local + dq_carry).astype(bf16).reshape(span, nheads * width)
    dk_flat = (dk_local + dk_carry).astype(bf16).reshape(span, nheads * width)
    dims = (((1,), (1,)), ((), ()))
    term = lax.dot_general(w_query, dq_flat, dims, preferred_element_type=f32)
    summed = lax.psum_scatter(
        (term + lax.dot_general(w_key, dk_flat, dims, preferred_element_type=f32)).astype(
            jnp.bfloat16
        ),
        "head",
        scatter_dimension=0,
        tiled=True,
    ).astype(jnp.float32)
    return summed.astype(bf16)


def solution(mesh):
    torus = Mesh(
        mesh.devices.reshape(8, 4, 2, mesh.shape["head"]), ("seq_0", "seq_1", "seq_2", "head")
    )
    return jax.shard_map(
        shards,
        mesh=torus,
        in_specs=(
            P(SEQ, "head"),
            P(SEQ, "head"),
            P(SEQ, "head"),
            P(SEQ, "head"),
            P(SEQ, "head"),
            P(None, "head"),
            P(None, "head"),
        ),
        out_specs=P("head", SEQ),
        check_vma=False,
    )
```

profile of v0, /device:TPU:8, one launch (start us, length us, event | category | flops | bytes accessed | tf_op | source)
XLA Modules:
  0.0 238.1 jit_solution(6543333811605289557)
XLA Ops:
  6.5 0.7 reshape.167
  7.2 0.9 reduce-window.6
  8.7 1.8 all-gather.2
  10.5 9.7 %all-gather.3 = f32[4,1,3]{2,1,0:T(1,128)S(1)} all-gather(f32[1,1,3]{2,1,0:T(1,128)S(1)} %get-tuple-element.43), channel_id=1, replica_groups=mesh['seq_0'=8,'seq_1'=4,'seq_2'=2,'head'=12] {'seq_1'}, dimensions={0}, use_global_device_ids=true | all-gather | bytes 60 | tf_op jit(solution)/shard_map/all_gather | solution.py:21
  20.4 1.1 copy.91
  21.4 1.1 copy.87
  22.5 1.1 copy.81
  23.8 2.1 all-gather
  25.9 1.1 copy.82
  27.1 2.1 all-gather.1
  29.9 14.5 %all_gather.58 = f32[4,3,128,128]{3,2,1,0:T(8,128)S(1)} all-gather(f32[1,3,128,128]{3,2,1,0:T(8,128)S(1)} %bitcast_add_fusion.4), channel_id=1, replica_groups=mesh['seq_0'=8,'seq_1'=4,'seq_2'=2,'head'=12] {'seq_1'}, dimensions={0}, use_global_device_ids=true | all-gather | bytes 983040 | tf_op jit(solution)/shard_map/all_gather | solution.py:21
  44.5 13.3 %all_gather.53 = f32[4,3,128,128]{3,2,1,0:T(8,128)S(1)} all-gather(f32[1,3,128,128]{3,2,1,0:T(8,128)S(1)} %bitcast_add_fusion.10), channel_id=1, replica_groups=mesh['seq_0'=8,'seq_1'=4,'seq_2'=2,'head'=12] {'seq_1'}, dimensions={0}, use_global_device_ids=true | all-gather | bytes 983040 | tf_op jit(solution)/shard_map/all_gather | solution.py:21
  57.9 0.9 multiply_add_fusion
  59.7 19.6 %all-gather.5 = f32[8,1,3]{2,1,0:T(1,128)S(1)} all-gather(f32[1,1,3]{2,1,0:T(1,128)S(1)} %get-tuple-element.29), channel_id=1, replica_groups=mesh['seq_0'=8,'seq_1'=4,'seq_2'=2,'head'=12] {'seq_0'}, dimensions={0}, use_global_device_ids=true | all-gather | bytes 108 | tf_op jit(solution)/shard_map/all_gather | solution.py:21
  79.2 13.3 %all-gather.4 = f32[8,1,3]{2,1,0:T(1,128)S(1)} all-gather(f32[1,1,3]{2,1,0:T(1,128)S(1)} %get-tuple-element.30), channel_id=1, replica_groups=mesh['seq_0'=8,'seq_1'=4,'seq_2'=2,'head'=12] {'seq_0'}, dimensions={0}, use_global_device_ids=true | all-gather | bytes 108 | tf_op jit(solution)/shard_map/all_gather | solution.py:21
  94.8 1.0 convolution_bitcast_fusion.1
  95.9 12.9 %all-gather.11.cloned.1.call-done = f32[8,3,128,128]{3,2,1,0:T(8,128)} async-done(((f32[1,3,128,128]{3,2,1,0:T(8,128)}), f32[8,3,128,128]{3,2,1,0:T(8,128)}) %all-gather.11.cloned.1.call-update) | async-done | bytes 1572880 | tf_op jit(solution)/shard_map/all_gather | solution.py:21
  108.7 2.0 fusion.4
  111.0 43.5 %all-gather.9.cloned.1.call-done = f32[8,3,128,128]{3,2,1,0:T(8,128)} async-done(((f32[1,3,128,128]{3,2,1,0:T(8,128)}), f32[8,3,128,128]{3,2,1,0:T(8,128)}) %all-gather.9.cloned.1.call-update) | async-done | bytes 1572880 | tf_op jit(solution)/shard_map/all_gather | solution.py:21
  154.7 2.3 fusion.9
  156.9 4.2 %fusion.59 = f32[256,6144]{1,0:T(8,128)S(1)} fusion(bf16[256,384]{0,1:T(8,128)(2,1)S(1)} %bitcast.386, bf16[6144,384]{1,0:T(8,128)(2,1)} %param.12), kind=kOutput, calls=%fused_computation.144 | convolution fusion | flops 1207959552 | bytes 11206656 | tf_op jit(solution)/shard_map/dot_general | solution.py:74
  161.2 3.5 %fusion.1 = bf16[6144,256]{0,1:T(8,128)(2,1)} fusion(f32[256,6144]{1,0:T(8,128)S(1)} %fusion.59, bf16[256,384]{0,1:T(8,128)(2,1)S(1)} %bitcast.379, bf16[6144,384]{1,0:T(8,128)(2,1)S(1)} %bitcast.374), kind=kOutput, calls=%fused_computation.2 | convolution fusion | flops 1211105280 | bytes 14352384 | tf_op jit(solution)/shard_map/dot_general | solution.py:76
  164.7 65.1 %reduce-scatter.2.cloned.1.call-done = bf16[512,256]{0,1:T(8,128)(2,1)} async-done(((bf16[6144,256]{0,1:T(8,128)(2,1)}), bf16[512,256]{0,1:T(8,128)(2,1)}) %reduce-scatter.2.cloned.1.call-update) | async-done | bytes 262160 | tf_op jit(solution)/shard_map/reduce_scatter | solution.py:75
  229.8 1.8 copy.95
  (82 shorter events, 5.3 us)
Async XLA Ops:
  6.5 102.2 %all-gather.11.cloned.1.call-start = ((), (), s32[]{:S(2)}) async-start(), calls=%async_computation.2 | async-start | bytes 1769472 | tf_op jit(solution)/shard_map/all_gather | solution.py:21
  10.5 49.1 %copy-start.2 = (f32[3]{0:T(128)}, f32[3]{0:T(128)S(1)}, u32[]{:S(2)}) copy-start(f32[3]{0:T(128)S(1)} %get-tuple-element.41) | copy-start | bytes 40
  20.3 39.3 %copy-start.9 = (f32[3]{0:T(128)}, f32[3]{0:T(128)S(1)}, u32[]{:S(2)}) copy-start(f32[3]{0:T(128)S(1)} %get-tuple-element.35) | copy-start | bytes 40
  20.3 39.3 %copy-start.11 = (f32[3]{0:T(128)}, f32[3]{0:T(128)S(1)}, u32[]{:S(2)}) copy-start(f32[3]{0:T(128)S(1)} %get-tuple-element.36) | copy-start | bytes 40
  20.3 39.3 %copy-start.13 = (f32[3]{0:T(128)}, f32[3]{0:T(128)S(1)}, u32[]{:S(2)}) copy-start(f32[3]{0:T(128)S(1)} %get-tuple-element.33) | copy-start | bytes 40
  29.8 49.4 %copy-start = (f32[3]{0:T(128)}, f32[3]{0:T(128)S(1)}, u32[]{:S(2)}) copy-start(f32[3]{0:T(128)S(1)} %get-tuple-element.38) | copy-start | bytes 40
  29.8 64.0 %copy-start.3 = (f32[3]{0:T(128)}, f32[3]{0:T(128)S(1)}, u32[]{:S(2)}) copy-start(f32[3]{0:T(128)S(1)} %get-tuple-element.37) | copy-start | bytes 40
  58.8 95.7 %all-gather.9.cloned.1.call-start = ((), (), s32[]{:S(2)}) async-start(), calls=%async_computation.1 | async-start | bytes 1769472 | tf_op jit(solution)/shard_map/all_gather | solution.py:21
  59.6 170.2 %reduce-scatter.2.cloned.1.call-start = ((), (), s32[]{:S(2)}) async-start(), calls=%async_computation.3 | async-start | bytes 3407872 | tf_op jit(solution)/shard_map/reduce_scatter | solution.py:75
  94.8 59.7 %copy-start.1 = (f32[3]{0:T(128)S(1)}, f32[3]{0:T(128)}, u32[]{:S(2)}) copy-start(f32[3]{0:T(128)} %copy-done) | copy-start | bytes 40
  95.8 58.8 %copy-start.5 = (f32[3]{0:T(128)S(1)}, f32[3]{0:T(128)}, u32[]{:S(2)}) copy-start(f32[3]{0:T(128)} %copy-done.4) | copy-start | bytes 40
  95.8 58.8 %copy-start.8 = (f32[3]{0:T(128)S(1)}, f32[3]{0:T(128)}, u32[]{:S(2)}) copy-start(f32[3]{0:T(128)} %copy-done.7) | copy-start | bytes 40
  95.8 58.8 %copy-start.10 = (f32[3]{0:T(128)S(1)}, f32[3]{0:T(128)}, u32[]{:S(2)}) copy-start(f32[3]{0:T(128)} %copy-done.9) | copy-start | bytes 40
  95.8 58.8 %copy-start.12 = (f32[3]{0:T(128)S(1)}, f32[3]{0:T(128)}, u32[]{:S(2)}) copy-start(f32[3]{0:T(128)} %copy-done.11) | copy-start | bytes 40
  95.8 58.8 %copy-start.14 = (f32[3]{0:T(128)S(1)}, f32[3]{0:T(128)}, u32[]{:S(2)}) copy-start(f32[3]{0:T(128)} %get-tuple-element.9) | copy-start | bytes 40
  95.8 58.8 %copy-start.15 = (f32[3]{0:T(128)S(1)}, f32[3]{0:T(128)}, u32[]{:S(2)}) copy-start(f32[3]{0:T(128)} %get-tuple-element.10) | copy-start | bytes 40
  95.8 58.8 %copy-start.16 = (f32[3]{0:T(128)S(1)}, f32[3]{0:T(128)}, u32[]{:S(2)}) copy-start(f32[3]{0:T(128)} %get-tuple-element.19) | copy-start | bytes 40
  95.8 58.8 %copy-start.17 = (f32[3]{0:T(128)S(1)}, f32[3]{0:T(128)}, u32[]{:S(2)}) copy-start(f32[3]{0:T(128)} %get-tuple-element.20) | copy-start | bytes 40
  95.8 58.8 %copy-start.18 = (f32[3]{0:T(128)S(1)}, f32[3]{0:T(128)}, u32[]{:S(2)}) copy-start(f32[3]{0:T(128)} %get-tuple-element.21) | copy-start | bytes 40
  95.8 58.8 %copy-start.19 = (f32[3]{0:T(128)S(1)}, f32[3]{0:T(128)}, u32[]{:S(2)}) copy-start(f32[3]{0:T(128)} %get-tuple-element.22) | copy-start | bytes 40
  95.8 58.8 %copy-start.20 = (f32[3]{0:T(128)S(1)}, f32[3]{0:T(128)}, u32[]{:S(2)}) copy-start(f32[3]{0:T(128)} %get-tuple-element.23) | copy-start | bytes 40
  95.8 58.8 %copy-start.21 = (f32[3]{0:T(128)S(1)}, f32[3]{0:T(128)}, u32[]{:S(2)}) copy-start(f32[3]{0:T(128)} %get-tuple-element.24) | copy-start | bytes 40
  95.8 58.8 %copy-start.22 = (f32[3]{0:T(128)S(1)}, f32[3]{0:T(128)}, u32[]{:S(2)}) copy-start(f32[3]{0:T(128)} %get-tuple-element.25) | copy-start | bytes 40
  95.9 58.8 %copy-start.23 = (f32[3]{0:T(128)S(1)}, f32[3]{0:T(128)}, u32[]{:S(2)}) copy-start(f32[3]{0:T(128)} %get-tuple-element.26) | copy-start | bytes 40
  (5 other events, 109.6 us)
Sparse Core Ops, SparseCore 0:
  58.9 49.7 all-gather.10
  111.1 43.3 all-gather.8
  164.8 64.9 reduce-scatter.1
where the time goes:
time: 238 us
  waiting for transfers between devices  122 us (51%)
  blocking collectives  76.4 us (32%)
  matrix products  14 us (6%)
  between operations  13.5 us (6%)
  local copies, waits for them, and re-layouts  7.33 us (3%)
  other arithmetic  4.61 us (2%)
    all_gather x8, blocking collectives, carried_in(): pieces = jax.tree.map(lambda part: lax.all_gather(part, axis), subtotal)  76.4 us
    reduce_scatter x1, waiting for transfers between devices, shards(): lax.psum_scatter((term + lax.dot_general(w_key, dk_flat, dims, preferred_...  65.1 us
    all_gather x2, waiting for transfers between devices, carried_in(): pieces = jax.tree.map(lambda part: lax.all_gather(part, axis), subtotal)  56.4 us
  transfers between devices with their start and end apart: 3, of which 3 were waited for; matrix products, arithmetic and copies ran while one was open for 2% of the time, Pallas kernels for 0%

commit v1 on v0

v1 whole, which is shorter than its diff:
```python
import functools

import jax
import jax.numpy as jnp
from jax import lax
from jax.experimental import pallas as pl
from jax.experimental.pallas import tpu as pltpu
from jax.sharding import Mesh
from jax.sharding import PartitionSpec as P

SEQ = ("seq_0", "seq_1", "seq_2")
F32 = jnp.float32
BF16 = jnp.bfloat16
MESH = pl.DeviceIdType.MESH
LANES = 128
PIECES = 4


def nn(a, b):
    return lax.dot_general(a, b, (((1,), (0,)), ((), ())), preferred_element_type=F32)


def nt(a, b):
    return lax.dot_general(a, b, (((1,), (1,)), ((), ())), preferred_element_type=F32)


def kernel(
    dims,
    q_hbm, k_hbm, v_hbm, g_hbm, ld_hbm, wq_hbm, wk_hbm,
    out_ref,
    q_v, k_v, v_v, g_v, ld_v, wq_v, wk_v,
    buf_a, rec_a, lbuf_a, lrec_a,
    exc, wgt, tot_b, rec_b, lbuf_b, lrec_b,
    buf_c, rec_c,
    loc, xt, sbuf, rbuf,
    in_sem,
    sa_sem, ra_sem, sla_sem, rla_sem,
    sb_sem, rb_sem, slb_sem, rlb_sem,
    sc_sem, rc_sem,
    sz_sem, rz_sem,
):
    ny, nr, nc, nz, nh, span, chunk = dims
    width = LANES
    hw = nh * width
    part = width // nr
    half = nz // 2
    rows = chunk // PIECES
    y = lax.axis_index("seq_0")
    r = lax.axis_index("seq_1") * nc + lax.axis_index("seq_2")
    z = lax.axis_index("head")

    def row_peer(p):
        return {"seq_1": p // nc, "seq_2": p % nc}

    loads = []
    for i, (src, dst) in enumerate(
        ((ld_hbm, ld_v), (k_hbm, k_v), (v_hbm, v_v), (q_hbm, q_v), (g_hbm, g_v), (wq_hbm, wq_v), (wk_hbm, wk_v))
    ):
        load = pltpu.make_async_copy(src, dst, in_sem.at[i])
        load.start()
        loads.append(load)

    barrier = pltpu.get_barrier_semaphore()
    for i in range(1, nr):
        pl.semaphore_signal(barrier, inc=1, device_id=row_peer((r + i) % nr), device_id_type=MESH)
    for i in range(1, ny):
        pl.semaphore_signal(barrier, inc=1, device_id={"seq_0": (y + i) % ny}, device_id_type=MESH)
    for step in (1, nz - 1):
        pl.semaphore_signal(barrier, inc=1, device_id={"head": (z + step) % nz}, device_id_type=MESH)

    loads[0].wait()
    ld = jnp.concatenate([ld_v[...], jnp.zeros((8 - nh, span), F32)], axis=0)
    first = lax.broadcasted_iota(jnp.int32, (span, span), 0)
    second = lax.broadcasted_iota(jnp.int32, (span, span), 1)
    causal = first <= second
    cum = lax.dot_general(
        ld, causal.astype(F32), (((1,), (0,)), ((), ())), precision=lax.Precision.HIGHEST, preferred_element_type=F32
    )
    last = cum[:, span - 1 : span]
    lbuf_a[...] = jnp.broadcast_to(last, (8, LANES))
    up_decay = jnp.exp(cum)
    down_decay = jnp.exp(jnp.minimum(last - cum, 0.0))

    pl.semaphore_wait(barrier, nr + ny)

    def row_copy(src, dst, ssem, rsem, i, use_own):
        to = (r + i) % nr
        return pltpu.make_async_remote_copy(
            src_ref=src.at[to] if use_own else src,
            dst_ref=dst.at[r],
            send_sem=ssem.at[i - 1],
            recv_sem=rsem.at[r],
            device_id=row_peer(to),
            device_id_type=MESH,
        )

    def row_arrival(dst, rsem, i):
        frm = (r + i) % nr
        return pltpu.make_async_remote_copy(
            src_ref=dst.at[frm],
            dst_ref=dst.at[frm],
            send_sem=rsem.at[frm],
            recv_sem=rsem.at[frm],
            device_id=row_peer(frm),
            device_id_type=MESH,
        )

    sends = []

    def go(copy):
        copy.start()
        sends.append(copy)

    for i in range(1, nr):
        go(row_copy(lbuf_a, lrec_a, sla_sem, rla_sem, i, False))
    lrec_a[r] = lbuf_a[...]

    def flipped(ref):
        return ref[...].astype(F32).T

    loads[1].wait()
    k_t = flipped(k_v)
    loads[2].wait()
    for h in range(nh):
        cols = slice(h * width, (h + 1) * width)
        kw = (k_t[cols, :] * down_decay[h : h + 1, :]).astype(BF16)
        state = nn(kw, v_v[:, cols]).astype(BF16)
        buf_a[:, 0, h] = state.reshape(nr, part, width)
    loads[3].wait()
    q_t = flipped(q_v)
    loads[4].wait()
    for h in range(nh):
        cols = slice(h * width, (h + 1) * width)
        qw = (q_t[cols, :] * up_decay[h : h + 1, :]).astype(BF16)
        state = nn(qw, g_v[:, cols]).astype(BF16)
        buf_a[:, 1, h] = state.reshape(nr, part, width)
    for i in range(1, nr):
        go(row_copy(buf_a, rec_a, sa_sem, ra_sem, i, True))
    rec_a[r] = buf_a[r]

    for i in range(1, nr):
        row_arrival(lrec_a, rla_sem, i).wait_recv()
    ahead = jnp.zeros((8, LANES), F32)
    for p in range(nr):
        wgt[0, p] = jnp.exp(ahead)
        ahead = ahead + lrec_a[p]
    lbuf_b[...] = ahead
    behind = jnp.zeros((8, LANES), F32)
    for p in reversed(range(nr)):
        wgt[1, p] = jnp.exp(behind)
        behind = behind + lrec_a[p]

    def column_copy(src, dst, ssem, rsem, i, sided):
        return pltpu.make_async_remote_copy(
            src_ref=src.at[(y + i) // ny] if sided else src,
            dst_ref=dst.at[y],
            send_sem=ssem.at[i - 1],
            recv_sem=rsem.at[y],
            device_id={"seq_0": (y + i) % ny},
            device_id_type=MESH,
        )

    def column_arrival(dst, rsem, i):
        frm = (y + i) % ny
        return pltpu.make_async_remote_copy(
            src_ref=dst.at[frm],
            dst_ref=dst.at[frm],
            send_sem=rsem.at[frm],
            recv_sem=rsem.at[frm],
            device_id={"seq_0": frm},
            device_id_type=MESH,
        )

    for i in range(1, ny):
        go(column_copy(lbuf_b, lrec_b, slb_sem, rlb_sem, i, False))

    cum_t = cum.T
    k_b = k_t.astype(BF16)
    q_b = q_t.astype(BF16)

    def local_part(h):
        cols = slice(h * width, (h + 1) * width)
        gap = cum[h : h + 1, :] - cum_t[:, h : h + 1]
        decay = jnp.where(causal, jnp.exp(jnp.minimum(gap, 0.0)), 0.0)
        weighted = (nt(v_v[:, cols], g_v[:, cols]) * decay).astype(BF16)
        loc[0, h] = nn(k_b[cols, :], weighted)
        loc[1, h] = nt(q_b[cols, :], weighted)

    local_part(0)

    for i in range(1, nr):
        row_arrival(rec_a, ra_sem, i).wait_recv()
    for h in range(nh):
        run = jnp.zeros((part, width), F32)
        for p in range(nr):
            exc[0, p, h] = run
            run = jnp.exp(lrec_a[p, h : h + 1, :]) * run + rec_a[p, 0, h].astype(F32)
        tot_b[0, h] = run.astype(BF16)
        run = jnp.zeros((part, width), F32)
        for p in reversed(range(nr)):
            exc[1, p, h] = run
            run = jnp.exp(lrec_a[p, h : h + 1, :]) * run + rec_a[p, 1, h].astype(F32)
        tot_b[1, h] = run.astype(BF16)
    for i in range(1, ny):
        go(column_copy(tot_b, rec_b, sb_sem, rb_sem, i, True))

    for h in range(1, nh):
        local_part(h)

    for i in range(1, ny):
        column_arrival(lrec_b, rlb_sem, i).wait_recv()
    for i in range(1, ny):
        column_arrival(rec_b, rb_sem, i).wait_recv()

    def onward(p, run):
        decay = jnp.exp(lrec_b[p])
        return tuple(decay[h : h + 1, :] * run[h] + rec_b[p, h].astype(F32) for h in range(nh))

    empty = tuple(jnp.zeros((part, width), F32) for _ in range(nh))
    before = lax.fori_loop(0, y, onward, empty)
    after = lax.fori_loop(0, ny - 1 - y, lambda i, run: onward(ny - 1 - i, run), empty)
    for p in range(nr):
        for h in range(nh):
            buf_c[p, 0, h] = (wgt[0, p, h : h + 1, :] * before[h] + exc[0, p, h]).astype(BF16)
            buf_c[p, 1, h] = (wgt[1, p, h : h + 1, :] * after[h] + exc[1, p, h]).astype(BF16)
    for i in range(1, nr):
        go(row_copy(buf_c, rec_c, sc_sem, rc_sem, i, True))
    rec_c[r] = buf_c[r]
    g_t = flipped(g_v).astype(BF16)
    v_t = flipped(v_v).astype(BF16)
    for i in range(1, nr):
        row_arrival(rec_c, rc_sem, i).wait_recv()
    for h in range(nh):
        cols = slice(h * width, (h + 1) * width)
        state = rec_c[:, 0, h].reshape(width, width)
        xt[cols, :] = (loc[0, h] + nn(state, g_t[cols, :]) * up_decay[h : h + 1, :]).astype(BF16)
        state = rec_c[:, 1, h].reshape(width, width)
        xt[hw + h * width : hw + (h + 1) * width, :] = (
            loc[1, h] + nn(state, v_t[cols, :]) * down_decay[h : h + 1, :]
        ).astype(BF16)

    loads[5].wait()
    loads[6].wait()

    def own(dest, pc):
        span_rows = pl.ds(pl.multiple_of(dest * chunk + pc * rows, rows), rows)
        return nn(wq_v[span_rows, :], xt[0:hw, :]) + nn(wk_v[span_rows, :], xt[hw : 2 * hw, :])

    def ring_copy(way, step, pc):
        at = pl.ds(pc * rows, rows)
        return pltpu.make_async_remote_copy(
            src_ref=sbuf.at[way, step, at],
            dst_ref=rbuf.at[way, step, at],
            send_sem=sz_sem.at[way, step, pc],
            recv_sem=rz_sem.at[way, step, pc],
            device_id={"head": (z + (1 if way == 0 else nz - 1)) % nz},
            device_id_type=MESH,
        )

    def relay(way, step, pc, fresh):
        away = half - step
        dest = (z + (away if way == 0 else nz - away)) % nz
        value = own(dest, pc)
        at = pl.ds(pc * rows, rows)
        if not fresh:
            ring_copy(way, step - 1, pc).wait_recv()
            value = value + rbuf[way, step - 1, at, :].astype(F32)
        sbuf[way, step, at, :] = value.astype(BF16)
        ring_copy(way, step, pc).start()

    mid = PIECES // 2
    for i in range(mid):
        relay(0, 0, i, True)
        relay(1, 0, mid + i, True)
    for i in range(mid):
        relay(0, 1, mid + i, True)
        relay(1, 1, i, True)
    for i in range(mid):
        relay(0, 1, i, False)
        relay(1, 1, mid + i, False)

    def ring_step(step, carry):
        for i in range(PIECES):
            relay(0, step, (mid + i) % PIECES, False)
            relay(1, step, i, False)
        return carry

    lax.fori_loop(2, half, ring_step, 0)
    for i in range(PIECES):
        pc_up, pc_down = (mid + i) % PIECES, i
        for pc in (i,):
            at = pl.ds(pc * rows, rows)
            value = own(z, pc)
            ring_copy(0, half - 1, pc).wait_recv()
            ring_copy(1, half - 1, pc).wait_recv()
            value = value + rbuf[0, half - 1, at, :].astype(F32) + rbuf[1, half - 1, at, :].astype(F32)
            out_ref[at, :] = value.astype(BF16)

    for copy in sends:
        copy.wait_send()
    for way in range(2):
        for i in range(mid):
            ring_copy(way, 0, i + mid * way).wait_send()

    def drain(step, carry):
        for way in range(2):
            for pc in range(PIECES):
                ring_copy(way, step, pc).wait_send()
        return carry

    lax.fori_loop(1, half, drain, 0)


def shards(sizes, query_act, key_act, value_act, grad_output, log_decay, w_query, w_key):
    ny, nx, nc, nz = sizes
    span = query_act.shape[0]
    nh = log_decay.shape[1]
    width = query_act.shape[1] // nh
    hw = nh * width
    nr = nx * nc
    part = width // nr
    half = nz // 2
    features = w_query.shape[0]
    chunk = features // nz
    dims = (ny, nr, nc, nz, nh, span, chunk)
    vmem = pltpu.VMEM
    dma = pltpu.SemaphoreType.DMA
    scratch = [
        vmem((span, hw), BF16), vmem((span, hw), BF16), vmem((span, hw), BF16), vmem((span, hw), BF16),
        vmem((nh, span), F32), vmem((features, hw), BF16), vmem((features, hw), BF16),
        vmem((nr, 2, nh, part, width), BF16), vmem((nr, 2, nh, part, width), BF16),
        vmem((8, LANES), F32), vmem((nr, 8, LANES), F32),
        vmem((2, nr, nh, part, width), F32), vmem((2, nr, 8, LANES), F32),
        vmem((2, nh, part, width), BF16), vmem((ny, nh, part, width), BF16),
        vmem((8, LANES), F32), vmem((ny, 8, LANES), F32),
        vmem((nr, 2, nh, part, width), BF16), vmem((nr, 2, nh, part, width), BF16),
        vmem((2, nh, width, span), F32), vmem((2 * hw, span), BF16),
        vmem((2, half, chunk, span), BF16), vmem((2, half, chunk, span), BF16),
        dma((7,)),
        dma((nr - 1,)), dma((nr,)), dma((nr - 1,)), dma((nr,)),
        dma((ny - 1,)), dma((ny,)), dma((ny - 1,)), dma((ny,)),
        dma((nr - 1,)), dma((nr,)),
        dma((2, half, PIECES)), dma((2, half, PIECES)),
    ]
    hbm = pl.BlockSpec(memory_space=pl.ANY)
    return pl.pallas_call(
        functools.partial(kernel, dims),
        out_shape=jax.ShapeDtypeStruct((chunk, span), BF16),
        in_specs=[hbm] * 7,
        out_specs=pl.BlockSpec(memory_space=pltpu.VMEM),
        scratch_shapes=scratch,
        compiler_params=pltpu.CompilerParams(
            collective_id=0, has_side_effects=True, vmem_limit_bytes=60 * 1024 * 1024
        ),
        name="attention_backward",
    )(query_act, key_act, value_act, grad_output, log_decay.T, w_query, w_key)


def build(torus):
    sizes = tuple(torus.shape[a] for a in SEQ + ("head",))
    return jax.shard_map(
        functools.partial(shards, sizes),
        mesh=torus,
        in_specs=(
            P(SEQ, "head"),
            P(SEQ, "head"),
            P(SEQ, "head"),
            P(SEQ, "head"),
            P(SEQ, "head"),
            P(None, "head"),
            P(None, "head"),
        ),
        out_specs=P("head", SEQ),
        check_vma=False,
    )


def solution(mesh):
    torus = Mesh(
        mesh.devices.reshape(8, 4, 2, mesh.shape["head"]), ("seq_0", "seq_1", "seq_2", "head")
    )
    return build(torus)
```

time: 238 us -> 72.7 us (0.31)
  the two profiles are of different devices: /device:TPU:8 before, /device:TPU:1 now
where the time goes in v1:
time: 72.7 us; the launch traced here: 72.6 us
  Pallas kernels  70.9 us (98%)
  local copies, waits for them, and re-layouts  1.67 us (2%)
    pallas_call x1, Pallas kernels, shards(): pl.pallas_call(functools.partial(kernel, dims), out_shape=jax.ShapeDtypeS...  70.9 us
    unnamed x1, local copies, waits for them, and re-layouts  1.67 us

profile of v1, /device:TPU:1, one launch (start us, length us, event | category | flops | bytes accessed | tf_op | source)
XLA Modules:
  0.0 72.6 jit_solution(8997831616976819717)
XLA Ops:
  0.0 70.9 %attention_backward.1 = bf16[512,256]{1,0:T(8,128)(2,1)} custom-call(bf16[256,384]{1,0:T(8,128)(2,1)} %q_hbm.1, bf16[256,384]{1,0:T(8,128)(2,1)} %k_hbm.1, bf16[256,384]{1,0:T(8,128)(2,1)} %v_hbm.1, bf16[256,384]{1,0:T(8,128)(2,1)} %g_hbm.1, f32[3,256]{1,0:T(4,128)} %bitcast.1, bf16[6144,384]{1,0:T(8,128)(2,1)} %wq_hbm.1, bf16[6144,384]{1,0:T(8,128)(2,1)} %wk_hbm.1), custom_call_target="tpu_custom_call" | custom-call | tf_op jit(solution)/shard_map/attention_backward/pallas_call | solution.py:346
  70.9 1.7 %copy.9 = bf16[512,256]{1,0:T(8,128)(2,1)} copy(bf16[512,256]{1,0:T(8,128)(2,1)} %attention_backward.1) | data formatting | bytes 524288

commit v2 on v1

--- a/solution.py
+++ b/solution.py
@@ -30,7 +30,7 @@
     out_ref,
     q_v, k_v, v_v, g_v, ld_v, wq_v, wk_v,
     buf_a, rec_a, lbuf_a, lrec_a,
-    exc, wgt, tot_b, rec_b, lbuf_b, lrec_b,
+    exc, wgt, wgt_b, tot_b, rec_b, lbuf_b, lrec_b,
     buf_c, rec_c,
     loc, xt, sbuf, rbuf,
     in_sem,
@@ -83,14 +83,26 @@
 
     pl.semaphore_wait(barrier, nr + ny)
 
-    def row_copy(src, dst, ssem, rsem, i, use_own):
-        to = (r + i) % nr
-        return pltpu.make_async_remote_copy(
-            src_ref=src.at[to] if use_own else src,
-            dst_ref=dst.at[r],
-            send_sem=ssem.at[i - 1],
-            recv_sem=rsem.at[r],
-            device_id=row_peer(to),
+    def row_copy(src, dst, ssem, rsem, i):
+        return pltpu.make_async_remote_copy(
+            src_ref=src, dst_ref=dst, send_sem=ssem, recv_sem=rsem,
+            device_id=row_peer((r + i) % nr), device_id_type=MESH,
+        )
+
+    def column_copy(src, dst, ssem, rsem, i):
+        return pltpu.make_async_remote_copy(
+            src_ref=src, dst_ref=dst, send_sem=ssem, recv_sem=rsem,
+            device_id={"seq_0": (y + i) % ny}, device_id_type=MESH,
+        )
+
+    def column_arrival(dst, rsem, i):
+        frm = (y + i) % ny
+        return pltpu.make_async_remote_copy(
+            src_ref=dst.at[frm],
+            dst_ref=dst.at[frm],
+            send_sem=rsem.at[frm],
+            recv_sem=rsem.at[frm],
+            device_id={"seq_0": frm},
             device_id_type=MESH,
         )
 
@@ -112,132 +124,115 @@
         sends.append(copy)
 
     for i in range(1, nr):
-        go(row_copy(lbuf_a, lrec_a, sla_sem, rla_sem, i, False))
+        go(row_copy(lbuf_a, lrec_a.at[r], sla_sem.at[i - 1], rla_sem.at[r], i))
     lrec_a[r] = lbuf_a[...]
 
     def flipped(ref):
         return ref[...].astype(F32).T
+
+    def head(h):
+        return slice(h * width, (h + 1) * width)
 
     loads[1].wait()
     k_t = flipped(k_v)
     loads[2].wait()
-    for h in range(nh):
-        cols = slice(h * width, (h + 1) * width)
-        kw = (k_t[cols, :] * down_decay[h : h + 1, :]).astype(BF16)
-        state = nn(kw, v_v[:, cols]).astype(BF16)
-        buf_a[:, 0, h] = state.reshape(nr, part, width)
     loads[3].wait()
     q_t = flipped(q_v)
     loads[4].wait()
     for h in range(nh):
-        cols = slice(h * width, (h + 1) * width)
-        qw = (q_t[cols, :] * up_decay[h : h + 1, :]).astype(BF16)
-        state = nn(qw, g_v[:, cols]).astype(BF16)
-        buf_a[:, 1, h] = state.reshape(nr, part, width)
-    for i in range(1, nr):
-        go(row_copy(buf_a, rec_a, sa_sem, ra_sem, i, True))
-    rec_a[r] = buf_a[r]
+        kw = (k_t[head(h), :] * down_decay[h : h + 1, :]).astype(BF16)
+        qw = (q_t[head(h), :] * up_decay[h : h + 1, :]).astype(BF16)
+        buf_a[h, :, 0] = nn(kw, v_v[:, head(h)]).astype(BF16).reshape(nr, part, width)
+        buf_a[h, :, 1] = nn(qw, g_v[:, head(h)]).astype(BF16).reshape(nr, part, width)
+        for i in range(1, nr):
+            go(row_copy(buf_a.at[h, (r + i) % nr], rec_a.at[h, r], sa_sem.at[h, i - 1], ra_sem.at[h, r], i))
+        rec_a[h, r] = buf_a[h, r]
 
     for i in range(1, nr):
         row_arrival(lrec_a, rla_sem, i).wait_recv()
     ahead = jnp.zeros((8, LANES), F32)
     for p in range(nr):
         wgt[0, p] = jnp.exp(ahead)
+        wgt[2, p] = jnp.exp(lrec_a[p])
         ahead = ahead + lrec_a[p]
     lbuf_b[...] = ahead
+    for i in range(1, ny):
+        go(column_copy(lbuf_b, lrec_b.at[y], slb_sem.at[i - 1], rlb_sem.at[y], i))
     behind = jnp.zeros((8, LANES), F32)
     for p in reversed(range(nr)):
         wgt[1, p] = jnp.exp(behind)
         behind = behind + lrec_a[p]
 
-    def column_copy(src, dst, ssem, rsem, i, sided):
-        return pltpu.make_async_remote_copy(
-            src_ref=src.at[(y + i) // ny] if sided else src,
-            dst_ref=dst.at[y],
-            send_sem=ssem.at[i - 1],
-            recv_sem=rsem.at[y],
-            device_id={"seq_0": (y + i) % ny},
-            device_id_type=MESH,
-        )
-
-    def column_arrival(dst, rsem, i):
-        frm = (y + i) % ny
-        return pltpu.make_async_remote_copy(
-            src_ref=dst.at[frm],
-            dst_ref=dst.at[frm],
-            send_sem=rsem.at[frm],
-            recv_sem=rsem.at[frm],
-            device_id={"seq_0": frm},
-            device_id_type=MESH,
-        )
-
-    for i in range(1, ny):
-        go(column_copy(lbuf_b, lrec_b, slb_sem, rlb_sem, i, False))
-
     cum_t = cum.T
     k_b = k_t.astype(BF16)
     q_b = q_t.astype(BF16)
 
     def local_part(h):
-        cols = slice(h * width, (h + 1) * width)
         gap = cum[h : h + 1, :] - cum_t[:, h : h + 1]
         decay = jnp.where(causal, jnp.exp(jnp.minimum(gap, 0.0)), 0.0)
-        weighted = (nt(v_v[:, cols], g_v[:, cols]) * decay).astype(BF16)
-        loc[0, h] = nn(k_b[cols, :], weighted)
-        loc[1, h] = nt(q_b[cols, :], weighted)
+        weighted = (nt(v_v[:, head(h)], g_v[:, head(h)]) * decay).astype(BF16)
+        loc[0, h] = nn(k_b[head(h), :], weighted)
+        loc[1, h] = nt(q_b[head(h), :], weighted)
 
     local_part(0)
 
-    for i in range(1, nr):
-        row_arrival(rec_a, ra_sem, i).wait_recv()
     for h in range(nh):
+        for i in range(1, nr):
+            row_arrival(rec_a.at[h], ra_sem.at[h], i).wait_recv()
         run = jnp.zeros((part, width), F32)
         for p in range(nr):
-            exc[0, p, h] = run
-            run = jnp.exp(lrec_a[p, h : h + 1, :]) * run + rec_a[p, 0, h].astype(F32)
-        tot_b[0, h] = run.astype(BF16)
+            exc[h, 0, p] = run
+            run = wgt[2, p, h : h + 1, :] * run + rec_a[h, p, 0].astype(F32)
+        tot_b[h, 0] = run.astype(BF16)
         run = jnp.zeros((part, width), F32)
         for p in reversed(range(nr)):
-            exc[1, p, h] = run
-            run = jnp.exp(lrec_a[p, h : h + 1, :]) * run + rec_a[p, 1, h].astype(F32)
-        tot_b[1, h] = run.astype(BF16)
+            exc[h, 1, p] = run
+            run = wgt[2, p, h : h + 1, :] * run + rec_a[h, p, 1].astype(F32)
+        tot_b[h, 1] = run.astype(BF16)
+        for i in range(1, ny):
+            go(column_copy(tot_b.at[h, (y + i) // ny], rec_b.at[h, y], sb_sem.at[h, i - 1], rb_sem.at[h, y], i))
+        rec_b[h, y] = jnp.zeros((part, width), BF16)
+
+    lrec_b[y] = jnp.zeros((8, LANES), F32)
     for i in range(1, ny):
-        go(column_copy(tot_b, rec_b, sb_sem, rb_sem, i, True))
+        column_arrival(lrec_b, rlb_sem, i).wait_recv()
+    ahead = jnp.zeros((8, LANES), F32)
+    for p in reversed(range(ny)):
+        wgt_b[0, p] = jnp.where(p < y, jnp.exp(ahead), 0.0)
+        ahead = ahead + jnp.where(p < y, lrec_b[p], 0.0)
+    behind = jnp.zeros((8, LANES), F32)
+    for p in range(ny):
+        wgt_b[1, p] = jnp.where(p > y, jnp.exp(behind), 0.0)
+        behind = behind + jnp.where(p > y, lrec_b[p], 0.0)
 
     for h in range(1, nh):
         local_part(h)
-
-    for i in range(1, ny):
-        column_arrival(lrec_b, rlb_sem, i).wait_recv()
-    for i in range(1, ny):
-        column_arrival(rec_b, rb_sem, i).wait_recv()
-
-    def onward(p, run):
-        decay = jnp.exp(lrec_b[p])
-        return tuple(decay[h : h + 1, :] * run[h] + rec_b[p, h].astype(F32) for h in range(nh))
-
-    empty = tuple(jnp.zeros((part, width), F32) for _ in range(nh))
-    before = lax.fori_loop(0, y, onward, empty)
-    after = lax.fori_loop(0, ny - 1 - y, lambda i, run: onward(ny - 1 - i, run), empty)
-    for p in range(nr):
-        for h in range(nh):
-            buf_c[p, 0, h] = (wgt[0, p, h : h + 1, :] * before[h] + exc[0, p, h]).astype(BF16)
-            buf_c[p, 1, h] = (wgt[1, p, h : h + 1, :] * after[h] + exc[1, p, h]).astype(BF16)
-    for i in range(1, nr):
-        go(row_copy(buf_c, rec_c, sc_sem, rc_sem, i, True))
-    rec_c[r] = buf_c[r]
     g_t = flipped(g_v).astype(BF16)
     v_t = flipped(v_v).astype(BF16)
-    for i in range(1, nr):
-        row_arrival(rec_c, rc_sem, i).wait_recv()
+
     for h in range(nh):
-        cols = slice(h * width, (h + 1) * width)
-        state = rec_c[:, 0, h].reshape(width, width)
-        xt[cols, :] = (loc[0, h] + nn(state, g_t[cols, :]) * up_decay[h : h + 1, :]).astype(BF16)
-        state = rec_c[:, 1, h].reshape(width, width)
-        xt[hw + h * width : hw + (h + 1) * width, :] = (
-            loc[1, h] + nn(state, v_t[cols, :]) * down_decay[h : h + 1, :]
-        ).astype(BF16)
+        for i in range(1, ny):
+            column_arrival(rec_b.at[h], rb_sem.at[h], i).wait_recv()
+        before = jnp.zeros((part, width), F32)
+        after = jnp.zeros((part, width), F32)
+        for p in range(ny):
+            term = rec_b[h, p].astype(F32)
+            before = before + wgt_b[0, p, h : h + 1, :] * term
+            after = after + wgt_b[1, p, h : h + 1, :] * term
+        for p in range(nr):
+            buf_c[h, p, 0] = (wgt[0, p, h : h + 1, :] * before + exc[h, 0, p]).astype(BF16)
+            buf_c[h, p, 1] = (wgt[1, p, h : h + 1, :] * after + exc[h, 1, p]).astype(BF16)
+        for i in range(1, nr):
+            go(row_copy(buf_c.at[h, (r + i) % nr], rec_c.at[h, r], sc_sem.at[h, i - 1], rc_sem.at[h, r], i))
+        rec_c[h, r] = buf_c[h, r]
+
+    for h in range(nh):
+        for i in range(1, nr):
+            row_arrival(rec_c.at[h], rc_sem.at[h], i).wait_recv()
+        state = rec_c[h, :, 0].reshape(width, width)
+        xt[head(h), :] = (loc[0, h] + nn(state, g_t[head(h), :]) * up_decay[h : h + 1, :]).astype(BF16)
+        state = rec_c[h, :, 1].reshape(width, width)
+        xt[head(nh + h), :] = (loc[1, h] + nn(state, v_t[head(h), :]) * down_decay[h : h + 1, :]).astype(BF16)
 
     loads[5].wait()
     loads[6].wait()
@@ -286,15 +281,14 @@
         return carry
 
     lax.fori_loop(2, half, ring_step, 0)
+    for pc in range(PIECES):
+        out_ref[pl.ds(pc * rows, rows), :] = own(z, pc)
     for i in range(PIECES):
-        pc_up, pc_down = (mid + i) % PIECES, i
-        for pc in (i,):
-            at = pl.ds(pc * rows, rows)
-            value = own(z, pc)
-            ring_copy(0, half - 1, pc).wait_recv()
-            ring_copy(1, half - 1, pc).wait_recv()
-            value = value + rbuf[0, half - 1, at, :].astype(F32) + rbuf[1, half - 1, at, :].astype(F32)
-            out_ref[at, :] = value.astype(BF16)
+        pc = i // 2 + mid * (i % 2)
+        at = pl.ds(pc * rows, rows)
+        for way in (i % 2, 1 - i % 2):
+            ring_copy(1 - way, half - 1, pc).wait_recv()
+            out_ref[at, :] += rbuf[1 - way, half - 1, at, :].astype(F32)
 
     for copy in sends:
         copy.wait_send()
@@ -328,32 +322,33 @@
     scratch = [
         vmem((span, hw), BF16), vmem((span, hw), BF16), vmem((span, hw), BF16), vmem((span, hw), BF16),
         vmem((nh, span), F32), vmem((features, hw), BF16), vmem((features, hw), BF16),
-        vmem((nr, 2, nh, part, width), BF16), vmem((nr, 2, nh, part, width), BF16),
+        vmem((nh, nr, 2, part, width), BF16), vmem((nh, nr, 2, part, width), BF16),
         vmem((8, LANES), F32), vmem((nr, 8, LANES), F32),
-        vmem((2, nr, nh, part, width), F32), vmem((2, nr, 8, LANES), F32),
-        vmem((2, nh, part, width), BF16), vmem((ny, nh, part, width), BF16),
+        vmem((nh, 2, nr, part, width), F32), vmem((3, nr, 8, LANES), F32), vmem((2, ny, 8, LANES), F32),
+        vmem((nh, 2, part, width), BF16), vmem((nh, ny, part, width), BF16),
         vmem((8, LANES), F32), vmem((ny, 8, LANES), F32),
-        vmem((nr, 2, nh, part, width), BF16), vmem((nr, 2, nh, part, width), BF16),
+        vmem((nh, nr, 2, part, width), BF16), vmem((nh, nr, 2, part, width), BF16),
         vmem((2, nh, width, span), F32), vmem((2 * hw, span), BF16),
         vmem((2, half, chunk, span), BF16), vmem((2, half, chunk, span), BF16),
         dma((7,)),
-        dma((nr - 1,)), dma((nr,)), dma((nr - 1,)), dma((nr,)),
-        dma((ny - 1,)), dma((ny,)), dma((ny - 1,)), dma((ny,)),
-        dma((nr - 1,)), dma((nr,)),
+        dma((nh, nr - 1)), dma((nh, nr)), dma((nr - 1,)), dma((nr,)),
+        dma((nh, ny - 1)), dma((nh, ny)), dma((ny - 1,)), dma((ny,)),
+        dma((nh, nr - 1)), dma((nh, nr)),
         dma((2, half, PIECES)), dma((2, half, PIECES)),
     ]
     hbm = pl.BlockSpec(memory_space=pl.ANY)
-    return pl.pallas_call(
+    total = pl.pallas_call(
         functools.partial(kernel, dims),
-        out_shape=jax.ShapeDtypeStruct((chunk, span), BF16),
+        out_shape=pltpu.VMEM((chunk, span), F32),
         in_specs=[hbm] * 7,
         out_specs=pl.BlockSpec(memory_space=pltpu.VMEM),
         scratch_shapes=scratch,
         compiler_params=pltpu.CompilerParams(
-            collective_id=0, has_side_effects=True, vmem_limit_bytes=60 * 1024 * 1024
+            collective_id=0, has_side_effects=True, vmem_limit_bytes=56 * 1024 * 1024
         ),
         name="attention_backward",
     )(query_act, key_act, value_act, grad_output, log_decay.T, w_query, w_key)
+    return total.astype(BF16)
 
 
 def build(torus):

time: 72.7 us -> 70.1 us (0.964)
  Pallas kernels: 70.9 us -> 69.2 us
  local copies, waits for them, and re-layouts: 1.67 us -> 0 us
  other arithmetic: 0 us -> 0.73 us
    pallas_call x1, Pallas kernels: 70.9 us -> 69.2 us  [shards(): pl.pallas_call(functools.partial(kernel, dims), out_shape=pltpu.VMEM((chu...]
    unnamed x1 -> x0, local copies, waits for them, and re-layouts: 1.67 us -> none
    convert_element_type x0 -> x1, other arithmetic: none -> 0.73 us  [shards(): return total.astype(BF16)]
where the time goes in v2:
time: 70.1 us; the launch traced here: 70 us
  Pallas kernels  69.2 us (99%)
  other arithmetic  0.73 us (1%)
    pallas_call x1, Pallas kernels, shards(): pl.pallas_call(functools.partial(kernel, dims), out_shape=pltpu.VMEM((chu...  69.2 us

profile of v2, /device:TPU:1, one launch (start us, length us, event | category | flops | bytes accessed | tf_op | source)
XLA Modules:
  0.0 70.0 jit_solution(4411244452989913848)
XLA Ops:
  0.0 69.2 %attention_backward.1 = f32[512,256]{1,0:T(8,128)S(1)} custom-call(bf16[256,384]{1,0:T(8,128)(2,1)} %q_hbm.1, bf16[256,384]{1,0:T(8,128)(2,1)} %k_hbm.1, bf16[256,384]{1,0:T(8,128)(2,1)} %v_hbm.1, bf16[256,384]{1,0:T(8,128)(2,1)} %g_hbm.1, f32[3,256]{1,0:T(4,128)} %bitcast.1, bf16[6144,384]{1,0:T(8,128)(2,1)} %wq_hbm.1, bf16[6144,384]{1,0:T(8,128)(2,1)} %wk_hbm.1), custom_call_target="tpu_custom_call" | custom-call | tf_op jit(solution)/shard_map/attention_backward/pallas_call | solution.py:340
  69.2 0.7 %convert_element_type.3 = bf16[512,256]{1,0:T(8,128)(2,1)} convert(f32[512,256]{1,0:T(8,128)S(1)} %attention_backward.1) | non-fusion elementwise | flops 131072 | bytes 786432 | tf_op jit(solution)/shard_map/convert_element_type | solution.py:351

commit v3 on v2

--- a/solution.py
+++ b/solution.py
@@ -13,7 +13,7 @@
 BF16 = jnp.bfloat16
 MESH = pl.DeviceIdType.MESH
 LANES = 128
-PIECES = 4
+PIECES = 2
 
 
 def nn(a, b):
@@ -22,6 +22,10 @@
 
 def nt(a, b):
     return lax.dot_general(a, b, (((1,), (1,)), ((), ())), preferred_element_type=F32)
+
+
+def far_first(n):
+    return sorted(range(1, n), key=lambda i: abs(2 * i - n))
 
 
 def kernel(
@@ -57,14 +61,15 @@
         ((ld_hbm, ld_v), (k_hbm, k_v), (v_hbm, v_v), (q_hbm, q_v), (g_hbm, g_v), (wq_hbm, wq_v), (wk_hbm, wk_v))
     ):
         load = pltpu.make_async_copy(src, dst, in_sem.at[i])
+        loads.append(load)
+    for load in loads[:5]:
         load.start()
-        loads.append(load)
 
     barrier = pltpu.get_barrier_semaphore()
-    for i in range(1, nr):
+    for i in far_first(ny):
+        pl.semaphore_signal(barrier, inc=1, device_id={"seq_0": (y + i) % ny}, device_id_type=MESH)
+    for i in far_first(nr):
         pl.semaphore_signal(barrier, inc=1, device_id=row_peer((r + i) % nr), device_id_type=MESH)
-    for i in range(1, ny):
-        pl.semaphore_signal(barrier, inc=1, device_id={"seq_0": (y + i) % ny}, device_id_type=MESH)
     for step in (1, nz - 1):
         pl.semaphore_signal(barrier, inc=1, device_id={"head": (z + step) % nz}, device_id_type=MESH)
 
@@ -81,8 +86,6 @@
     up_decay = jnp.exp(cum)
     down_decay = jnp.exp(jnp.minimum(last - cum, 0.0))
 
-    pl.semaphore_wait(barrier, nr + ny)
-
     def row_copy(src, dst, ssem, rsem, i):
         return pltpu.make_async_remote_copy(
             src_ref=src, dst_ref=dst, send_sem=ssem, recv_sem=rsem,
@@ -123,10 +126,6 @@
         copy.start()
         sends.append(copy)
 
-    for i in range(1, nr):
-        go(row_copy(lbuf_a, lrec_a.at[r], sla_sem.at[i - 1], rla_sem.at[r], i))
-    lrec_a[r] = lbuf_a[...]
-
     def flipped(ref):
         return ref[...].astype(F32).T
 
@@ -139,12 +138,20 @@
     loads[3].wait()
     q_t = flipped(q_v)
     loads[4].wait()
+    for load in loads[5:]:
+        load.start()
     for h in range(nh):
         kw = (k_t[head(h), :] * down_decay[h : h + 1, :]).astype(BF16)
         qw = (q_t[head(h), :] * up_decay[h : h + 1, :]).astype(BF16)
         buf_a[h, :, 0] = nn(kw, v_v[:, head(h)]).astype(BF16).reshape(nr, part, width)
         buf_a[h, :, 1] = nn(qw, g_v[:, head(h)]).astype(BF16).reshape(nr, part, width)
-        for i in range(1, nr):
+
+    pl.semaphore_wait(barrier, nr + ny)
+    for i in far_first(nr):
+        go(row_copy(lbuf_a, lrec_a.at[r], sla_sem.at[i - 1], rla_sem.at[r], i))
+    lrec_a[r] = lbuf_a[...]
+    for h in range(nh):
+        for i in far_first(nr):
             go(row_copy(buf_a.at[h, (r + i) % nr], rec_a.at[h, r], sa_sem.at[h, i - 1], ra_sem.at[h, r], i))
         rec_a[h, r] = buf_a[h, r]
 
@@ -156,7 +163,7 @@
         wgt[2, p] = jnp.exp(lrec_a[p])
         ahead = ahead + lrec_a[p]
     lbuf_b[...] = ahead
-    for i in range(1, ny):
+    for i in far_first(ny):
         go(column_copy(lbuf_b, lrec_b.at[y], slb_sem.at[i - 1], rlb_sem.at[y], i))
     behind = jnp.zeros((8, LANES), F32)
     for p in reversed(range(nr)):
@@ -189,9 +196,14 @@
             exc[h, 1, p] = run
             run = wgt[2, p, h : h + 1, :] * run + rec_a[h, p, 1].astype(F32)
         tot_b[h, 1] = run.astype(BF16)
-        for i in range(1, ny):
+        for i in far_first(ny):
             go(column_copy(tot_b.at[h, (y + i) // ny], rec_b.at[h, y], sb_sem.at[h, i - 1], rb_sem.at[h, y], i))
         rec_b[h, y] = jnp.zeros((part, width), BF16)
+
+    for h in range(1, nh):
+        local_part(h)
+    g_t = flipped(g_v).astype(BF16)
+    v_t = flipped(v_v).astype(BF16)
 
     lrec_b[y] = jnp.zeros((8, LANES), F32)
     for i in range(1, ny):
@@ -205,11 +217,6 @@
         wgt_b[1, p] = jnp.where(p > y, jnp.exp(behind), 0.0)
         behind = behind + jnp.where(p > y, lrec_b[p], 0.0)
 
-    for h in range(1, nh):
-        local_part(h)
-    g_t = flipped(g_v).astype(BF16)
-    v_t = flipped(v_v).astype(BF16)
-
     for h in range(nh):
         for i in range(1, ny):
             column_arrival(rec_b.at[h], rb_sem.at[h], i).wait_recv()
@@ -222,7 +229,7 @@
         for p in range(nr):
             buf_c[h, p, 0] = (wgt[0, p, h : h + 1, :] * before + exc[h, 0, p]).astype(BF16)
             buf_c[h, p, 1] = (wgt[1, p, h : h + 1, :] * after + exc[h, 1, p]).astype(BF16)
-        for i in range(1, nr):
+        for i in far_first(nr):
             go(row_copy(buf_c.at[h, (r + i) % nr], rec_c.at[h, r], sc_sem.at[h, i - 1], rc_sem.at[h, r], i))
         rec_c[h, r] = buf_c[h, r]
 

time: 70.1 us -> 68.8 us (0.981)
  Pallas kernels: 69.2 us -> 67.9 us
    pallas_call x1, Pallas kernels: 69.2 us -> 67.9 us  [shards(): pl.pallas_call(functools.partial(kernel, dims), out_shape=pltpu.VMEM((chu...]
where the time goes in v3:
time: 68.8 us; the launch traced here: 68.7 us
  Pallas kernels  67.9 us (99%)
  other arithmetic  0.73 us (1%)
    pallas_call x1, Pallas kernels, shards(): pl.pallas_call(functools.partial(kernel, dims), out_shape=pltpu.VMEM((chu...  67.9 us

profile of v3, /device:TPU:1, one launch (start us, length us, event | category | flops | bytes accessed | tf_op | source)
XLA Modules:
  0.0 68.7 jit_solution(16179090416271199729)
XLA Ops:
  0.0 67.9 %attention_backward.1 = f32[512,256]{1,0:T(8,128)S(1)} custom-call(bf16[256,384]{1,0:T(8,128)(2,1)} %q_hbm.1, bf16[256,384]{1,0:T(8,128)(2,1)} %k_hbm.1, bf16[256,384]{1,0:T(8,128)(2,1)} %v_hbm.1, bf16[256,384]{1,0:T(8,128)(2,1)} %g_hbm.1, f32[3,256]{1,0:T(4,128)} %bitcast.1, bf16[6144,384]{1,0:T(8,128)(2,1)} %wq_hbm.1, bf16[6144,384]{1,0:T(8,128)(2,1)} %wk_hbm.1), custom_call_target="tpu_custom_call" | custom-call | tf_op jit(solution)/shard_map/attention_backward/pallas_call | solution.py:347
  68.0 0.7 %convert_element_type.3 = bf16[512,256]{1,0:T(8,128)(2,1)} convert(f32[512,256]{1,0:T(8,128)S(1)} %attention_backward.1) | non-fusion elementwise | flops 131072 | bytes 786432 | tf_op jit(solution)/shard_map/convert_element_type | solution.py:358

commit v4 on v3

--- a/solution.py
+++ b/solution.py
@@ -233,7 +233,7 @@
             go(row_copy(buf_c.at[h, (r + i) % nr], rec_c.at[h, r], sc_sem.at[h, i - 1], rc_sem.at[h, r], i))
         rec_c[h, r] = buf_c[h, r]
 
-    for h in range(nh):
+    def finish(h):
         for i in range(1, nr):
             row_arrival(rec_c.at[h], rc_sem.at[h], i).wait_recv()
         state = rec_c[h, :, 0].reshape(width, width)
@@ -241,8 +241,21 @@
         state = rec_c[h, :, 1].reshape(width, width)
         xt[head(nh + h), :] = (loc[1, h] + nn(state, v_t[head(h), :]) * down_decay[h : h + 1, :]).astype(BF16)
 
+    mid = PIECES // 2
+    most = (nh - 1) * width
+    far = (z + half) % nz
+
+    def some(pc, lo, hi):
+        span_rows = pl.ds(pl.multiple_of(far * chunk + pc * rows, rows), rows)
+        return nn(wq_v[span_rows, lo:hi], xt[lo:hi, :]) + nn(wk_v[span_rows, lo:hi], xt[hw + lo : hw + hi, :])
+
+    for h in range(nh - 1):
+        finish(h)
     loads[5].wait()
     loads[6].wait()
+    for pc in range(PIECES):
+        out_ref[pl.ds(pc * rows, rows), :] = some(pc, 0, most)
+    finish(nh - 1)
 
     def own(dest, pc):
         span_rows = pl.ds(pl.multiple_of(dest * chunk + pc * rows, rows), rows)
@@ -270,10 +283,12 @@
         sbuf[way, step, at, :] = value.astype(BF16)
         ring_copy(way, step, pc).start()
 
-    mid = PIECES // 2
     for i in range(mid):
-        relay(0, 0, i, True)
-        relay(1, 0, mid + i, True)
+        for way in range(2):
+            pc = mid * way + i
+            at = pl.ds(pc * rows, rows)
+            sbuf[way, 0, at, :] = (out_ref[at, :] + some(pc, most, hw)).astype(BF16)
+            ring_copy(way, 0, pc).start()
     for i in range(mid):
         relay(0, 1, mid + i, True)
         relay(1, 1, i, True)
@@ -290,6 +305,19 @@
     lax.fori_loop(2, half, ring_step, 0)
     for pc in range(PIECES):
         out_ref[pl.ds(pc * rows, rows), :] = own(z, pc)
+    for copy in sends:
+        copy.wait_send()
+    for way in range(2):
+        for i in range(mid):
+            ring_copy(way, 0, i + mid * way).wait_send()
+
+    def drain(step, carry):
+        for way in range(2):
+            for pc in range(PIECES):
+                ring_copy(way, step, pc).wait_send()
+        return carry
+
+    lax.fori_loop(1, half - 1, drain, 0)
     for i in range(PIECES):
         pc = i // 2 + mid * (i % 2)
         at = pl.ds(pc * rows, rows)
@@ -297,19 +325,9 @@
             ring_copy(1 - way, half - 1, pc).wait_recv()
             out_ref[at, :] += rbuf[1 - way, half - 1, at, :].astype(F32)
 
-    for copy in sends:
-        copy.wait_send()
     for way in range(2):
-        for i in range(mid):
-            ring_copy(way, 0, i + mid * way).wait_send()
-
-    def drain(step, carry):
-        for way in range(2):
-            for pc in range(PIECES):
-                ring_copy(way, step, pc).wait_send()
-        return carry
-
-    lax.fori_loop(1, half, drain, 0)
+        for pc in range(PIECES):
+            ring_copy(way, half - 1, pc).wait_send()
 
 
 def shards(sizes, query_act, key_act, value_act, grad_output, log_decay, w_query, w_key):

time: 68.8 us -> 68.5 us (level)
  no operation moved by 1% of the time
where the time goes in v4:
time: 68.5 us; the launch traced here: 68.4 us
  Pallas kernels  67.6 us (99%)
  other arithmetic  0.73 us (1%)
    pallas_call x1, Pallas kernels, shards(): pl.pallas_call(functools.partial(kernel, dims), out_shape=pltpu.VMEM((chu...  67.6 us

profile of v4, /device:TPU:1, one launch (start us, length us, event | category | flops | bytes accessed | tf_op | source)
XLA Modules:
  0.0 68.4 jit_solution(15581859120026264891)
XLA Ops:
  0.0 67.6 %attention_backward.1 = f32[512,256]{1,0:T(8,128)S(1)} custom-call(bf16[256,384]{1,0:T(8,128)(2,1)} %q_hbm.1, bf16[256,384]{1,0:T(8,128)(2,1)} %k_hbm.1, bf16[256,384]{1,0:T(8,128)(2,1)} %v_hbm.1, bf16[256,384]{1,0:T(8,128)(2,1)} %g_hbm.1, f32[3,256]{1,0:T(4,128)} %bitcast.1, bf16[6144,384]{1,0:T(8,128)(2,1)} %wq_hbm.1, bf16[6144,384]{1,0:T(8,128)(2,1)} %wk_hbm.1), custom_call_target="tpu_custom_call" | custom-call | tf_op jit(solution)/shard_map/attention_backward/pallas_call | solution.py:365
  67.6 0.7 %convert_element_type.3 = bf16[512,256]{1,0:T(8,128)(2,1)} convert(f32[512,256]{1,0:T(8,128)S(1)} %attention_backward.1) | non-fusion elementwise | flops 131072 | bytes 786432 | tf_op jit(solution)/shard_map/convert_element_type | solution.py:376

commit v5 on v4

--- a/solution.py
+++ b/solution.py
@@ -127,7 +127,7 @@
         sends.append(copy)
 
     def flipped(ref):
-        return ref[...].astype(F32).T
+        return ref[...].T
 
     def head(h):
         return slice(h * width, (h + 1) * width)
@@ -141,8 +141,8 @@
     for load in loads[5:]:
         load.start()
     for h in range(nh):
-        kw = (k_t[head(h), :] * down_decay[h : h + 1, :]).astype(BF16)
-        qw = (q_t[head(h), :] * up_decay[h : h + 1, :]).astype(BF16)
+        kw = (k_t[head(h), :].astype(F32) * down_decay[h : h + 1, :]).astype(BF16)
+        qw = (q_t[head(h), :].astype(F32) * up_decay[h : h + 1, :]).astype(BF16)
         buf_a[h, :, 0] = nn(kw, v_v[:, head(h)]).astype(BF16).reshape(nr, part, width)
         buf_a[h, :, 1] = nn(qw, g_v[:, head(h)]).astype(BF16).reshape(nr, part, width)
 
@@ -171,15 +171,13 @@
         behind = behind + lrec_a[p]
 
     cum_t = cum.T
-    k_b = k_t.astype(BF16)
-    q_b = q_t.astype(BF16)
 
     def local_part(h):
         gap = cum[h : h + 1, :] - cum_t[:, h : h + 1]
         decay = jnp.where(causal, jnp.exp(jnp.minimum(gap, 0.0)), 0.0)
         weighted = (nt(v_v[:, head(h)], g_v[:, head(h)]) * decay).astype(BF16)
-        loc[0, h] = nn(k_b[head(h), :], weighted)
-        loc[1, h] = nt(q_b[head(h), :], weighted)
+        loc[0, h] = nn(k_t[head(h), :], weighted)
+        loc[1, h] = nt(q_t[head(h), :], weighted)
 
     local_part(0)
 
@@ -202,8 +200,8 @@
 
     for h in range(1, nh):
         local_part(h)
-    g_t = flipped(g_v).astype(BF16)
-    v_t = flipped(v_v).astype(BF16)
+    g_t = flipped(g_v)
+    v_t = flipped(v_v)
 
     lrec_b[y] = jnp.zeros((8, LANES), F32)
     for i in range(1, ny):

time: 68.5 us -> 68.6 us (level)
  no operation moved by 1% of the time
where the time goes in v5:
time: 68.6 us; the launch traced here: 68.5 us
  Pallas kernels  67.7 us (99%)
  other arithmetic  0.73 us (1%)
    pallas_call x1, Pallas kernels, shards(): pl.pallas_call(functools.partial(kernel, dims), out_shape=pltpu.VMEM((chu...  67.7 us

profile of v5, /device:TPU:1, one launch (start us, length us, event | category | flops | bytes accessed | tf_op | source)
XLA Modules:
  0.0 68.5 jit_solution(5317815156596141146)
XLA Ops:
  0.0 67.7 %attention_backward.1 = f32[512,256]{1,0:T(8,128)S(1)} custom-call(bf16[256,384]{1,0:T(8,128)(2,1)} %q_hbm.1, bf16[256,384]{1,0:T(8,128)(2,1)} %k_hbm.1, bf16[256,384]{1,0:T(8,128)(2,1)} %v_hbm.1, bf16[256,384]{1,0:T(8,128)(2,1)} %g_hbm.1, f32[3,256]{1,0:T(4,128)} %bitcast.1, bf16[6144,384]{1,0:T(8,128)(2,1)} %wq_hbm.1, bf16[6144,384]{1,0:T(8,128)(2,1)} %wk_hbm.1), custom_call_target="tpu_custom_call" | custom-call | tf_op jit(solution)/shard_map/attention_backward/pallas_call | solution.py:363
  67.7 0.7 %convert_element_type.3 = bf16[512,256]{1,0:T(8,128)(2,1)} convert(f32[512,256]{1,0:T(8,128)S(1)} %attention_backward.1) | non-fusion elementwise | flops 131072 | bytes 786432 | tf_op jit(solution)/shard_map/convert_element_type | solution.py:374

commit v6 on v5

--- a/solution.py
+++ b/solution.py
@@ -138,8 +138,6 @@
     loads[3].wait()
     q_t = flipped(q_v)
     loads[4].wait()
-    for load in loads[5:]:
-        load.start()
     for h in range(nh):
         kw = (k_t[head(h), :].astype(F32) * down_decay[h : h + 1, :]).astype(BF16)
         qw = (q_t[head(h), :].astype(F32) * up_decay[h : h + 1, :]).astype(BF16)
@@ -197,6 +195,9 @@
         for i in far_first(ny):
             go(column_copy(tot_b.at[h, (y + i) // ny], rec_b.at[h, y], sb_sem.at[h, i - 1], rb_sem.at[h, y], i))
         rec_b[h, y] = jnp.zeros((part, width), BF16)
+
+    for load in loads[5:]:
+        load.start()
 
     for h in range(1, nh):
         local_part(h)

time: 68.6 us -> 68.6 us (level)
  no operation moved by 1% of the time
where the time goes in v6:
time: 68.6 us; the launch traced here: 68.5 us
  Pallas kernels  67.7 us (99%)
  other arithmetic  0.73 us (1%)
    pallas_call x1, Pallas kernels, shards(): pl.pallas_call(functools.partial(kernel, dims), out_shape=pltpu.VMEM((chu...  67.7 us

profile of v6, /device:TPU:1, one launch (start us, length us, event | category | flops | bytes accessed | tf_op | source)
XLA Modules:
  0.0 68.5 jit_solution(8830371723286501061)
XLA Ops:
  0.0 67.7 %attention_backward.1 = f32[512,256]{1,0:T(8,128)S(1)} custom-call(bf16[256,384]{1,0:T(8,128)(2,1)} %q_hbm.1, bf16[256,384]{1,0:T(8,128)(2,1)} %k_hbm.1, bf16[256,384]{1,0:T(8,128)(2,1)} %v_hbm.1, bf16[256,384]{1,0:T(8,128)(2,1)} %g_hbm.1, f32[3,256]{1,0:T(4,128)} %bitcast.1, bf16[6144,384]{1,0:T(8,128)(2,1)} %wq_hbm.1, bf16[6144,384]{1,0:T(8,128)(2,1)} %wk_hbm.1), custom_call_target="tpu_custom_call" | custom-call | tf_op jit(solution)/shard_map/attention_backward/pallas_call | solution.py:364
  67.7 0.7 %convert_element_type.3 = bf16[512,256]{1,0:T(8,128)(2,1)} convert(f32[512,256]{1,0:T(8,128)S(1)} %attention_backward.1) | non-fusion elementwise | flops 131072 | bytes 786432 | tf_op jit(solution)/shard_map/convert_element_type | solution.py:375
